TPU v7x, 32 devices: a whole 2x2x4 slice. The times are simulated.
32 devices in a mesh: node: 4 (over z), dom: 8 (over y, x, core).
Axes of the slice: x: 2, y: 2, z: 4, core: 2. Of those that a mesh axis runs over, the one named last changes fastest.
Arguments:
- probes: float32 [32, 16, 16, 128], P(None, 'dom'), may hold values from -24 to 24
- slope: float32 [16, 16, 128], P('dom'), may hold values from 4 to 6
- root: float32 [16, 16, 128], P('dom'), may hold values from 0.3 to 0.7
- damping: float32 [16, 16, 128], P('dom'), may hold values from 0.3 to 1.2
Outputs:
- moments: float32 [2, 2, 32, 16, 16, 128], P(None, None, 'node', 'dom')
- projections: float32 [2, 2, 32, 32], replicated
All inputs are finite; a program needn't handle non-finite values.
Results may differ from a plain program's by a relative error of at most 0.00013.
Values sent between devices are 32-bit elements; how exact they have to be, the bound alone decides.
A program may use at most 64 MiB of HBM per device.

v0:
```python
import math
import jax
import jax.numpy as jnp
from jax import lax
from jax.sharding import PartitionSpec as P

NODE_DEV = 2
SWEEPS = 8
CENTRE = 0.5
RADIUS = 2.0


def grid_step(source, fields, factor_re, factor_im):
    padded = jnp.pad(fields, ((0, 0), (0, 0), (1, 1), (1, 1), (1, 1)))
    total = padded[:, :, 2:, 1:-1, 1:-1] + padded[:, :, :-2, 1:-1, 1:-1]
    total = total + padded[:, :, 1:-1, 2:, 1:-1] + padded[:, :, 1:-1, :-2, 1:-1]
    total = total + padded[:, :, 1:-1, 1:-1, 2:] + padded[:, :, 1:-1, 1:-1, :-2]
    real_part = source + total[:, 0]
    imag_part = total[:, 1]
    return jnp.stack(
        [
            real_part * factor_re - imag_part * factor_im,
            real_part * factor_im + imag_part * factor_re,
        ],
        axis=1,
    )


def inverse_diagonal(shift_real, shift_imaginary, slope, root, damping, guard):
    zr_col = shift_real[:, None, None, None, None]
    zi_col = shift_imaginary[:, None, None, None, None]
    decay = jnp.exp(-zr_col)
    real_d = slope * (zr_col - root) + damping * (decay * jnp.cos(zi_col))
    imag_d = slope * zi_col - damping * (decay * jnp.sin(zi_col))
    scale = 1.0 / (real_d * real_d + imag_d * imag_d + guard)
    return (real_d * scale, -imag_d * scale)


def per_system(fields, weight_re, weight_im):
    a_col = weight_re[:, None, None, None]
    b_col = weight_im[:, None, None, None]
    return jnp.stack(
        [a_col * fields[:, 0] - b_col * fields[:, 1], a_col * fields[:, 1] + b_col * fields[:, 0]]
    )


def body(probes, slope, root, damping):
    vectors = probes.shape[0]
    planes = probes.shape[1]
    groups = lax.axis_size("node")
    total = NODE_DEV * groups
    first = (lax.axis_index("node") * NODE_DEV).astype(jnp.float32)
    dom_size = lax.axis_size("dom")
    count = NODE_DEV * vectors // dom_size
    replicated = jnp.broadcast_to(probes[None], (NODE_DEV,) + probes.shape).reshape(
        (NODE_DEV * vectors,) + probes.shape[1:]
    )
    own = lax.all_to_all(replicated, "dom", split_axis=0, concat_axis=1, tiled=True)
    slope_all, root_all, damping_all = (
        lax.all_gather(slope, "dom", axis=0, tiled=True),
        lax.all_gather(root, "dom", axis=0, tiled=True),
        lax.all_gather(damping, "dom", axis=0, tiled=True),
    )
    system = lax.axis_index("dom") * count + jnp.arange(count)
    position = first + (system // vectors).astype(jnp.float32)
    theta = 2.0 * math.pi * (position + 0.5) / total
    shift_real = CENTRE + RADIUS * jnp.cos(theta)
    shift_imaginary = RADIUS * jnp.sin(theta)
    qre, qim = inverse_diagonal(
        shift_real, shift_imaginary, slope_all[None], root_all[None], damping_all[None], 0.0
    )
    qre = qre[:, 0]
    qim = qim[:, 0]
    fields = jnp.stack([own * qre, own * qim], axis=1)
    for sweep in range(SWEEPS):
        fields = grid_step(own, fields, qre, qim)
    weight_re = RADIUS * jnp.cos(theta) / total
    weight_im = RADIUS * jnp.sin(theta) / total
    shifted_re = weight_re * shift_real - weight_im * shift_imaginary
    shifted_im = weight_re * shift_imaginary + weight_im * shift_real
    terms = jnp.stack(
        [per_system(fields, weight_re, weight_im), per_system(fields, shifted_re, shifted_im)]
    )
    back = lax.all_to_all(terms, "dom", split_axis=3, concat_axis=2, tiled=True)
    local = jnp.sum(back.reshape((2, 2, NODE_DEV, vectors) + probes.shape[1:]), axis=2)
    flat = local.reshape(4 * vectors, -1)
    basis = probes.reshape(vectors, -1)
    partial_value = lax.dot_general(
        flat,
        basis,
        (((1,), (1,)), ((), ())),
        precision=lax.Precision.HIGHEST,
        preferred_element_type=jnp.float32,
    )
    cells = planes * probes.shape[2] * probes.shape[3] * lax.axis_size("dom")
    projections = lax.psum(partial_value.reshape(2, 2, vectors, vectors) / cells, ("node", "dom"))
    summed = lax.psum(local, "node")
    share = vectors // groups
    moments = lax.dynamic_slice_in_dim(summed, lax.axis_index("node") * share, share, 2)
    return (moments, projections)


def solution(mesh):
    in_specs = (
        P(None, "dom", None, None),
        P("dom", None, None),
        P("dom", None, None),
        P("dom", None, None),
    )
    out_specs = (P(None, None, "node", "dom", None, None), P())
    return jax.shard_map(body, mesh=mesh, in_specs=in_specs, out_specs=out_specs, check_vma=False)
```

profile of v0, /device:TPU:0, one launch (start us, length us, event | category | flops | bytes accessed | tf_op | source)
XLA Modules:
  0.0 260.8 jit_solution(6893673430703613702)
XLA Ops:
  9.4 5.2 %all-to-all-start = ((f32[64,2,16,128]{3,2,1,0:T(8,128)}), f32[64,2,16,128]{3,2,1,0:T(8,128)S(1)}, u32[]{:S(2)}, u32[]{:S(2)}) async-start(f32[64,2,16,128]{3,2,1,0:T(8,128)} %bitcast), calls=%async_computation | async-start | bytes 2097152 | tf_op jit(solution)/shard_map/all_to_all | solution.py:58
  14.6 18.8 %all_gather.9 = f32[16,16,128]{2,1,0:T(8,128)S(1)} all-gather(f32[2,16,128]{2,1,0:T(8,128)S(1)} %copy-done.2), channel_id=1, replica_groups=mesh['node'=4,'dom'=8] {'dom'}, dimensions={0}, use_global_device_ids=true | all-gather | bytes 147456 | tf_op jit(solution)/shard_map/all_gather | solution.py:60
  33.4 8.3 %all_gather.10 = f32[16,16,128]{2,1,0:T(8,128)S(1)} all-gather(f32[2,16,128]{2,1,0:T(8,128)S(1)} %copy-done.3), channel_id=1, replica_groups=mesh['node'=4,'dom'=8] {'dom'}, dimensions={0}, use_global_device_ids=true | all-gather | bytes 147456 | tf_op jit(solution)/shard_map/all_gather | solution.py:61
  41.7 9.1 %all_gather.11 = f32[16,16,128]{2,1,0:T(8,128)S(1)} all-gather(f32[2,16,128]{2,1,0:T(8,128)S(1)} %copy-done.4), channel_id=1, replica_groups=mesh['node'=4,'dom'=8] {'dom'}, dimensions={0}, use_global_device_ids=true | all-gather | bytes 147456 | tf_op jit(solution)/shard_map/all_gather | solution.py:62
  51.6 2.6 select_maximum_fusion.7
  54.2 3.3 %slice_add_fusion.35 = f32[8,2,16,16,128]{4,3,2,0,1:T(8,128)S(1)} fusion(f32[8,2,18,18,130]{4,3,2,0,1:T(8,128)S(1)} %select_maximum_fusion.7), kind=kLoop, calls=%fused_computation.56 | loop fusion | flops 2621440 | bytes 14680064 | tf_op jit(solution)/shard_map/add | solution.py:17
  58.3 2.4 select_maximum_fusion.6
  60.7 3.3 %slice_add_fusion.30 = f32[8,2,16,16,128]{4,3,2,0,1:T(8,128)S(1)} fusion(f32[8,2,18,18,130]{4,3,2,0,1:T(8,128)S(1)} %select_maximum_fusion.6), kind=kLoop, calls=%fused_computation.51 | loop fusion | flops 2621440 | bytes 14680064 | tf_op jit(solution)/shard_map/add | solution.py:17
  64.7 2.4 select_maximum_fusion.5
  67.1 3.3 %slice_add_fusion.25 = f32[8,2,16,16,128]{4,3,2,0,1:T(8,128)S(1)} fusion(f32[8,2,18,18,130]{4,3,2,0,1:T(8,128)S(1)} %select_maximum_fusion.5), kind=kLoop, calls=%fused_computation.46 | loop fusion | flops 2621440 | bytes 14680064 | tf_op jit(solution)/shard_map/add | solution.py:17
  71.2 2.4 select_maximum_fusion.4
  73.6 3.3 %slice_add_fusion.20 = f32[8,2,16,16,128]{4,3,2,0,1:T(8,128)S(1)} fusion(f32[8,2,18,18,130]{4,3,2,0,1:T(8,128)S(1)} %select_maximum_fusion.4), kind=kLoop, calls=%fused_computation.41 | loop fusion | flops 2621440 | bytes 14680064 | tf_op jit(solution)/shard_map/add | solution.py:17
  77.6 2.6 select_maximum_fusion.3
  80.2 3.3 %slice_add_fusion.15 = f32[8,2,16,16,128]{4,3,2,0,1:T(8,128)S(1)} fusion(f32[8,2,18,18,130]{4,3,2,0,1:T(8,128)S(1)} %select_maximum_fusion.3), kind=kLoop, calls=%fused_computation.36 | loop fusion | flops 2621440 | bytes 14680064 | tf_op jit(solution)/shard_map/add | solution.py:17
  84.3 2.4 select_maximum_fusion.2
  86.7 3.3 %slice_add_fusion.10 = f32[8,2,16,16,128]{4,3,2,0,1:T(8,128)S(1)} fusion(f32[8,2,18,18,130]{4,3,2,0,1:T(8,128)S(1)} %select_maximum_fusion.2), kind=kLoop, calls=%fused_computation.31 | loop fusion | flops 2621440 | bytes 14680064 | tf_op jit(solution)/shard_map/add | solution.py:17
  90.8 2.4 select_maximum_fusion.1
  93.1 3.3 %slice_add_fusion.5 = f32[8,2,16,16,128]{4,3,2,0,1:T(8,128)S(1)} fusion(f32[8,2,18,18,130]{4,3,2,0,1:T(8,128)S(1)} %select_maximum_fusion.1), kind=kLoop, calls=%fused_computation.26 | loop fusion | flops 2621440 | bytes 14680064 | tf_op jit(solution)/shard_map/add | solution.py:17
  97.2 2.4 select_maximum_fusion
  99.6 3.5 %slice_add_fusion = f32[8,2,16,16,128]{4,3,2,0,1:T(8,128)S(1)} fusion(f32[8,2,18,18,130]{4,3,2,0,1:T(8,128)S(1)} %select_maximum_fusion), kind=kLoop, calls=%fused_computation.21 | loop fusion | flops 2621440 | bytes 14680064 | tf_op jit(solution)/shard_map/add | solution.py:17
  106.0 51.6 %all_to_all.36 = f32[2,2,8,16,16,128]{5,4,2,1,0,3:T(8,128)S(1)} all-to-all(f32[2,2,8,16,16,128]{5,4,2,1,0,3:T(8,128)S(1)} %copy.17), channel_id=1, replica_groups=mesh['node'=4,'dom'=8] {'dom'}, dimensions={3} | all-to-all | bytes 8388608 | tf_op jit(solution)/shard_map/all_to_all | solution.py:84
  159.2 3.1 %fusion.10 = f32[2,2,32,32]{3,2,1,0:T(8,128)S(1)} fusion(f32[2,2,32,2,16,128]{5,4,3,2,1,0:T(8,128)S(1)} %bitcast_reduce_fusion, f32[32,2,16,128,1,1]{3,2,1,0,5,4:T(8,128)S(1)} %bitcast.53), kind=kOutput, calls=%fused_computation.66 | convolution fusion | flops 201330688 | bytes 2637824 | tf_op jit(solution)/shard_map/dot_general | solution.py:88
  163.1 42.9 %psum.15 = f32[2,2,32,32]{3,2,1,0:T(8,128)} all-reduce(f32[2,2,32,32]{3,2,1,0:T(8,128)S(1)} %fusion.10), channel_id=1, replica_groups=mesh['node'=4,'dom'=8] {'node','dom'}, use_global_device_ids=true, to_apply=%region_2.3 | all-reduce | flops 4096 | bytes 32768 | tf_op jit(solution)/shard_map/psum | solution.py:96
  206.0 46.1 %all-reduce.10.cloned.1.call-done = f32[2,2,32,2,16,128]{5,4,3,2,1,0:T(8,128)} async-done(((f32[2,2,32,2,16,128]{5,4,3,2,1,0:T(8,128)}), f32[2,2,32,2,16,128]{5,4,3,2,1,0:T(8,128)}) %all-reduce.10.cloned.1.call-update) | async-done | bytes 2097168 | tf_op jit(solution)/shard_map/psum | solution.py:97
  (33 shorter events, 15.5 us)
Async XLA Ops:
  7.2 7.4 %copy-start.2 = (f32[2,16,128]{2,1,0:T(8,128)S(1)}, f32[2,16,128]{2,1,0:T(8,128)}, u32[]{:S(2)}) copy-start(f32[2,16,128]{2,1,0:T(8,128)} %param.5) | copy-start | bytes 49156
  7.2 26.2 %copy-start.3 = (f32[2,16,128]{2,1,0:T(8,128)S(1)}, f32[2,16,128]{2,1,0:T(8,128)}, u32[]{:S(2)}) copy-start(f32[2,16,128]{2,1,0:T(8,128)} %param.6) | copy-start | bytes 49156
  7.2 34.5 %copy-start.4 = (f32[2,16,128]{2,1,0:T(8,128)S(1)}, f32[2,16,128]{2,1,0:T(8,128)}, u32[]{:S(2)}) copy-start(f32[2,16,128]{2,1,0:T(8,128)} %param.7) | copy-start | bytes 49156
  9.4 41.5 %all-to-all-start = ((f32[64,2,16,128]{3,2,1,0:T(8,128)}), f32[64,2,16,128]{3,2,1,0:T(8,128)S(1)}, u32[]{:S(2)}, u32[]{:S(2)}) async-start(f32[64,2,16,128]{3,2,1,0:T(8,128)} %bitcast), calls=%async_computation | async-start | bytes 2097152 | tf_op jit(solution)/shard_map/all_to_all | solution.py:58
  158.2 1.0 copy-start.1
  158.7 3.6 %copy-start = (f32[2,2,32,2,16,128]{5,4,3,2,1,0:T(8,128)}, f32[2,2,32,2,16,128]{5,4,3,2,1,0:T(8,128)S(1)}, u32[]{:S(2)}) copy-start(f32[2,2,32,2,16,128]{5,4,3,2,1,0:T(8,128)S(1)} %bitcast_reduce_fusion) | copy-start | bytes 6291460
  162.3 89.8 %all-reduce.10.cloned.1.call-start = ((), (), s32[]{:S(2)}) async-start(), calls=%async_computation.2 | async-start | bytes 4194304 | tf_op jit(solution)/shard_map/psum | solution.py:97
Sparse Core Ops, SparseCore 0:
  165.5 86.5 all-reduce.9
where the time goes:
time: 261 us
  blocking collectives  131 us (50%)
  other arithmetic  54.8 us (21%)
  waiting for transfers between devices  46.8 us (18%)
  between operations  14.3 us (5%)
  local copies, waits for them, and re-layouts  5.8 us (2%)
  starting transfers between devices  5.24 us (2%)
  matrix products  3.08 us (1%)
    all_to_all x1, blocking collectives, body(): back = lax.all_to_all(terms, 'dom', split_axis=3, concat_axis=2, tiled=True)  51.6 us
    psum x1, waiting for transfers between devices, body(): summed = lax.psum(local, 'node')  46.1 us
    psum x1, blocking collectives, body(): lax.psum(partial_value.reshape(2, 2, vectors, vectors) / cells, ('node',...  42.9 us
    add x8, other arithmetic, grid_step(): total = total + padded[:, :, 1:-1, 1:-1, 2:] + padded[:, :, 1:-1, 1:-1, :-2]  26.4 us
    all_gather x1, blocking collectives, body(): lax.all_gather(slope, 'dom', axis=0, tiled=True)  18.8 us
    another operation x7, other arithmetic, grid_step(): jnp.stack([real_part * factor_re - imag_part * factor_im, real_part * fac...  16.9 us
    all_gather x1, blocking collectives, body(): lax.all_gather(damping, 'dom', axis=0, tiled=True)  9.1 us
    all_gather x1, blocking collectives, body(): lax.all_gather(root, 'dom', axis=0, tiled=True)  8.31 us
  transfers between devices with their start and end apart: 2, of which 1 were waited for; matrix products, arithmetic and copies ran while one was open for 0% of the time, Pallas kernels for 0%

commit v1 on v0

--- a/solution.py
+++ b/solution.py
@@ -57,7 +57,9 @@
     )
     own = lax.all_to_all(replicated, "dom", split_axis=0, concat_axis=1, tiled=True)
     slope_all, root_all, damping_all = (
-        lax.all_gather(slope, "dom", axis=0, tiled=True),
+        jnp.concatenate(
+            lax.all_to_all(jnp.stack([slope] * lax.axis_size("dom")), "dom", 0, 0), axis=0
+        ),
         lax.all_gather(root, "dom", axis=0, tiled=True),
         lax.all_gather(damping, "dom", axis=0, tiled=True),
     )

time: 261 us -> 263 us (level)
  blocking collectives: 131 us -> 113 us
  waiting for transfers between devices: 46.8 us -> 62.1 us
  starting transfers between devices: 5.24 us -> 8.61 us
    all_gather x1 -> x0, blocking collectives: 18.8 us -> none  [body(): lax.all_gather(slope, 'dom', axis=0, tiled=True)]
    all_to_all x1, waiting for transfers between devices: 0.01 us -> 15.3 us  [body(): lax.all_to_all(replicated, 'dom', split_axis=0, concat_axis=1, tiled=True)]
    all_to_all x0 -> x1, starting transfers between devices: none -> 3.37 us  [body(): lax.all_to_all(jnp.stack([slope] * lax.axis_size('dom')), 'dom', 0, 0)]
  transfers between devices with their start and end apart: 2 -> 3, of which waited for: 1 -> 2; matrix products, arithmetic and copies ran while one was open for 0% -> 0% of each run, Pallas kernels for 0% -> 0%
where the time goes in v1:
time: 263 us
  blocking collectives  113 us (43%)
  waiting for transfers between devices  62.1 us (24%)
  other arithmetic  54.9 us (21%)
  between operations  14.4 us (5%)
  starting transfers between devices  8.61 us (3%)
  local copies, waits for them, and re-layouts  6.45 us (2%)
  matrix products  3.07 us (1%)
    all_to_all x1, blocking collectives, body(): back = lax.all_to_all(terms, 'dom', split_axis=3, concat_axis=2, tiled=True)  51.6 us
    psum x1, waiting for transfers between devices, body(): summed = lax.psum(local, 'node')  46.1 us
    psum x1, blocking collectives, body(): lax.psum(partial_value.reshape(2, 2, vectors, vectors) / cells, ('node',...  42.9 us
    add x8, other arithmetic, grid_step(): total = total + padded[:, :, 1:-1, 1:-1, 2:] + padded[:, :, 1:-1, 1:-1, :-2]  26.4 us
    another operation x7, other arithmetic, grid_step(): jnp.stack([real_part * factor_re - imag_part * factor_im, real_part * fac...  16.9 us
    all_to_all x1, waiting for transfers between devices, body(): lax.all_to_all(replicated, 'dom', split_axis=0, concat_axis=1, tiled=True)  15.3 us
    all_gather x1, blocking collectives, body(): lax.all_gather(root, 'dom', axis=0, tiled=True)  9.64 us
    all_gather x1, blocking collectives, body(): lax.all_gather(damping, 'dom', axis=0, tiled=True)  9.16 us
  transfers between devices with their start and end apart: 3, of which 2 were waited for; matrix products, arithmetic and copies ran while one was open for 0% of the time, Pallas kernels for 0%

profile of v1, /device:TPU:0, one launch (start us, length us, event | category | flops | bytes accessed | tf_op | source)
XLA Modules:
  0.0 262.7 jit_solution(8294647504986737883)
XLA Ops:
  9.4 5.2 %all-to-all-start = ((f32[64,2,16,128]{3,2,1,0:T(8,128)}), f32[64,2,16,128]{3,2,1,0:T(8,128)S(1)}, u32[]{:S(2)}, u32[]{:S(2)}) async-start(f32[64,2,16,128]{3,2,1,0:T(8,128)} %bitcast), calls=%async_computation | async-start | bytes 2097152 | tf_op jit(solution)/shard_map/all_to_all | solution.py:58
  14.6 15.3 %all-to-all-done = f32[64,2,16,128]{3,2,1,0:T(8,128)S(1)} async-done(((f32[64,2,16,128]{3,2,1,0:T(8,128)}), f32[64,2,16,128]{3,2,1,0:T(8,128)S(1)}, u32[]{:S(2)}, u32[]{:S(2)}) %all-to-all-start) | async-done | bytes 1048608 | tf_op jit(solution)/shard_map/all_to_all | solution.py:58
  30.6 3.4 %all-to-all-start.1 = ((f32[8,2,16,128]{3,2,1,0:T(8,128)}), f32[8,2,16,128]{3,2,1,0:T(8,128)S(1)}, u32[]{:S(2)}, u32[]{:S(2)}) async-start(f32[8,2,16,128]{3,2,1,0:T(8,128)} %stack.28), calls=%async_computation.1 | async-start | bytes 262144 | tf_op jit(solution)/shard_map/all_to_all | solution.py:61
  34.0 9.6 %all_gather.6 = f32[16,16,128]{2,1,0:T(8,128)S(1)} all-gather(f32[2,16,128]{2,1,0:T(8,128)S(1)} %copy-done.3), channel_id=1, replica_groups=mesh['node'=4,'dom'=8] {'dom'}, dimensions={0}, use_global_device_ids=true | all-gather | bytes 147456 | tf_op jit(solution)/shard_map/all_gather | solution.py:63
  43.7 9.2 %all_gather.7 = f32[16,16,128]{2,1,0:T(8,128)S(1)} all-gather(f32[2,16,128]{2,1,0:T(8,128)S(1)} %copy-done.4), channel_id=1, replica_groups=mesh['node'=4,'dom'=8] {'dom'}, dimensions={0}, use_global_device_ids=true | all-gather | bytes 147456 | tf_op jit(solution)/shard_map/all_gather | solution.py:64
  53.6 2.6 select_maximum_fusion.7
  56.1 3.3 %slice_add_fusion.35 = f32[8,2,16,16,128]{4,3,2,0,1:T(8,128)S(1)} fusion(f32[8,2,18,18,130]{4,3,2,0,1:T(8,128)S(1)} %select_maximum_fusion.7), kind=kLoop, calls=%fused_computation.56 | loop fusion | flops 2621440 | bytes 14680064 | tf_op jit(solution)/shard_map/add | solution.py:17
  60.2 2.4 select_maximum_fusion.6
  62.6 3.3 %slice_add_fusion.30 = f32[8,2,16,16,128]{4,3,2,0,1:T(8,128)S(1)} fusion(f32[8,2,18,18,130]{4,3,2,0,1:T(8,128)S(1)} %select_maximum_fusion.6), kind=kLoop, calls=%fused_computation.51 | loop fusion | flops 2621440 | bytes 14680064 | tf_op jit(solution)/shard_map/add | solution.py:17
  66.7 2.4 select_maximum_fusion.5
  69.0 3.3 %slice_add_fusion.25 = f32[8,2,16,16,128]{4,3,2,0,1:T(8,128)S(1)} fusion(f32[8,2,18,18,130]{4,3,2,0,1:T(8,128)S(1)} %select_maximum_fusion.5), kind=kLoop, calls=%fused_computation.46 | loop fusion | flops 2621440 | bytes 14680064 | tf_op jit(solution)/shard_map/add | solution.py:17
  73.1 2.4 select_maximum_fusion.4
  75.5 3.3 %slice_add_fusion.20 = f32[8,2,16,16,128]{4,3,2,0,1:T(8,128)S(1)} fusion(f32[8,2,18,18,130]{4,3,2,0,1:T(8,128)S(1)} %select_maximum_fusion.4), kind=kLoop, calls=%fused_computation.41 | loop fusion | flops 2621440 | bytes 14680064 | tf_op jit(solution)/shard_map/add | solution.py:17
  79.6 2.6 select_maximum_fusion.3
  82.2 3.3 %slice_add_fusion.15 = f32[8,2,16,16,128]{4,3,2,0,1:T(8,128)S(1)} fusion(f32[8,2,18,18,130]{4,3,2,0,1:T(8,128)S(1)} %select_maximum_fusion.3), kind=kLoop, calls=%fused_computation.36 | loop fusion | flops 2621440 | bytes 14680064 | tf_op jit(solution)/shard_map/add | solution.py:17
  86.2 2.4 select_maximum_fusion.2
  88.6 3.3 %slice_add_fusion.10 = f32[8,2,16,16,128]{4,3,2,0,1:T(8,128)S(1)} fusion(f32[8,2,18,18,130]{4,3,2,0,1:T(8,128)S(1)} %select_maximum_fusion.2), kind=kLoop, calls=%fused_computation.31 | loop fusion | flops 2621440 | bytes 14680064 | tf_op jit(solution)/shard_map/add | solution.py:17
  92.7 2.4 select_maximum_fusion.1
  95.1 3.3 %slice_add_fusion.5 = f32[8,2,16,16,128]{4,3,2,0,1:T(8,128)S(1)} fusion(f32[8,2,18,18,130]{4,3,2,0,1:T(8,128)S(1)} %select_maximum_fusion.1), kind=kLoop, calls=%fused_computation.26 | loop fusion | flops 2621440 | bytes 14680064 | tf_op jit(solution)/shard_map/add | solution.py:17
  101.5 3.5 %slice_add_fusion = f32[8,2,16,16,128]{4,3,2,0,1:T(8,128)S(1)} fusion(f32[8,2,18,18,130]{4,3,2,0,1:T(8,128)S(1)} %select_maximum_fusion), kind=kLoop, calls=%fused_computation.21 | loop fusion | flops 2621440 | bytes 14680064 | tf_op jit(solution)/shard_map/add | solution.py:17
  108.0 51.6 %all_to_all.41 = f32[2,2,8,16,16,128]{5,4,2,1,0,3:T(8,128)S(1)} all-to-all(f32[2,2,8,16,16,128]{5,4,2,1,0,3:T(8,128)S(1)} %copy.17), channel_id=1, replica_groups=mesh['node'=4,'dom'=8] {'dom'}, dimensions={3} | all-to-all | bytes 8388608 | tf_op jit(solution)/shard_map/all_to_all | solution.py:86
  161.2 3.1 %fusion.10 = f32[2,2,32,32]{3,2,1,0:T(8,128)S(1)} fusion(f32[2,2,32,2,16,128]{5,4,3,2,1,0:T(8,128)S(1)} %bitcast_reduce_fusion, f32[32,2,16,128,1,1]{3,2,1,0,5,4:T(8,128)S(1)} %bitcast.63), kind=kOutput, calls=%fused_computation.66 | convolution fusion | flops 201330688 | bytes 2637824 | tf_op jit(solution)/shard_map/dot_general | solution.py:90
  165.0 42.9 %psum.15 = f32[2,2,32,32]{3,2,1,0:T(8,128)} all-reduce(f32[2,2,32,32]{3,2,1,0:T(8,128)S(1)} %fusion.10), channel_id=1, replica_groups=mesh['node'=4,'dom'=8] {'node','dom'}, use_global_device_ids=true, to_apply=%region_2.3 | all-reduce | flops 4096 | bytes 32768 | tf_op jit(solution)/shard_map/psum | solution.py:98
  207.9 46.1 %all-reduce.10.cloned.1.call-done = f32[2,2,32,2,16,128]{5,4,3,2,1,0:T(8,128)} async-done(((f32[2,2,32,2,16,128]{5,4,3,2,1,0:T(8,128)}), f32[2,2,32,2,16,128]{5,4,3,2,1,0:T(8,128)}) %all-reduce.10.cloned.1.call-update) | async-done | bytes 2097168 | tf_op jit(solution)/shard_map/psum | solution.py:99
  (35 shorter events, 18.6 us)
Async XLA Ops:
  7.2 22.8 %copy-start.2 = (f32[2,16,128]{2,1,0:T(8,128)S(1)}, f32[2,16,128]{2,1,0:T(8,128)}, u32[]{:S(2)}) copy-start(f32[2,16,128]{2,1,0:T(8,128)} %param.5) | copy-start | bytes 49156
  7.2 26.9 %copy-start.3 = (f32[2,16,128]{2,1,0:T(8,128)S(1)}, f32[2,16,128]{2,1,0:T(8,128)}, u32[]{:S(2)}) copy-start(f32[2,16,128]{2,1,0:T(8,128)} %param.6) | copy-start | bytes 49156
  7.2 36.5 %copy-start.4 = (f32[2,16,128]{2,1,0:T(8,128)S(1)}, f32[2,16,128]{2,1,0:T(8,128)}, u32[]{:S(2)}) copy-start(f32[2,16,128]{2,1,0:T(8,128)} %param.7) | copy-start | bytes 49156
  9.4 20.6 %all-to-all-start = ((f32[64,2,16,128]{3,2,1,0:T(8,128)}), f32[64,2,16,128]{3,2,1,0:T(8,128)S(1)}, u32[]{:S(2)}, u32[]{:S(2)}) async-start(f32[64,2,16,128]{3,2,1,0:T(8,128)} %bitcast), calls=%async_computation | async-start | bytes 2097152 | tf_op jit(solution)/shard_map/all_to_all | solution.py:58
  30.6 22.3 %all-to-all-start.1 = ((f32[8,2,16,128]{3,2,1,0:T(8,128)}), f32[8,2,16,128]{3,2,1,0:T(8,128)S(1)}, u32[]{:S(2)}, u32[]{:S(2)}) async-start(f32[8,2,16,128]{3,2,1,0:T(8,128)} %stack.28), calls=%async_computation.1 | async-start | bytes 262144 | tf_op jit(solution)/shard_map/all_to_all | solution.py:61
  160.1 1.0 copy-start.1
  160.7 3.6 %copy-start = (f32[2,2,32,2,16,128]{5,4,3,2,1,0:T(8,128)}, f32[2,2,32,2,16,128]{5,4,3,2,1,0:T(8,128)S(1)}, u32[]{:S(2)}) copy-start(f32[2,2,32,2,16,128]{5,4,3,2,1,0:T(8,128)S(1)} %bitcast_reduce_fusion) | copy-start | bytes 6291460
  164.3 89.8 %all-reduce.10.cloned.1.call-start = ((), (), s32[]{:S(2)}) async-start(), calls=%async_computation.3 | async-start | bytes 4194304 | tf_op jit(solution)/shard_map/psum | solution.py:99
Sparse Core Ops, SparseCore 0:
  167.4 86.5 all-reduce.9
